TPU v7x, 256 devices: a whole 4x4x8 slice. The times are simulated.
256 devices in a mesh: ctx: 16 (over x, y), head: 16 (over z, core).
Axes of the slice: x: 4, y: 4, z: 8, core: 2. Of those that a mesh axis runs over, the one named last changes fastest.
Arguments:
- tokens: bfloat16 [16384, 4096], P('ctx', 'head'), may hold values from -6 to 6
- doc_ids: int32 [16384], P('ctx'), may hold values from 0 to 7, never falling along the last dimension, each value on 1 to 8192 neighbouring positions
- w_feat: bfloat16 [4096, 1024], P(None, 'head'), may hold values from -0.09375 to 0.09375
- w_value: bfloat16 [4096, 4096], P(None, 'head'), may hold values from -0.09375 to 0.09375
- w_window: bfloat16 [4096, 8192], P(None, 'head'), may hold values from -4 to 4
- w_out: bfloat16 [4096, 4096], P('head'), may hold values from -0.09375 to 0.09375
Outputs:
- layer_out: bfloat16 [16384, 4096], P('ctx', 'head')
Inputs may be any that keep to these rules, and one draw needn't show every extreme that they name: `doc_ids`: document ids never fall along the sequence; each of the 8 documents has 1 to 8192 tokens, and one has exactly 8192.
All inputs are finite; a program needn't handle non-finite values.
Results may differ from a plain program's by a relative error of at most 0.019.
Values may be sent and summed in bfloat16 or wider, within the bound.
A program may use at most 128 MiB of HBM per device.

v0:
```python
import jax
import jax.numpy as jnp
from jax import lax
from jax.sharding import PartitionSpec as P

HEAD_DIM = 128
FEAT = 16
WIN = 64


def entering(x, axis, join, neutral):
    place = lax.axis_index(axis)
    gathered = jax.tree.map(
        lambda a, kind: lax.all_gather(a.astype(kind), axis), x, (jnp.bfloat16, jnp.bfloat16)
    )
    state = jax.tree.map(lambda a, e: jnp.zeros_like(a) + jnp.asarray(e, a.dtype), x, neutral)

    def one(step, state):
        return join(
            state,
            jax.tree.map(
                lambda a, own: lax.dynamic_index_in_dim(a, step, 0, False).astype(own.dtype),
                gathered,
                x,
            ),
        )

    return lax.fori_loop(0, place, one, state)


def shifted(x, axis, by):
    devices = lax.axis_size(axis)
    pairs = [(i, i + by) for i in range(devices) if 0 <= i + by < devices]
    return lax.ppermute(x, axis, pairs)


def feature_map(projected):
    widened = projected.astype(jnp.float32)
    products = widened[..., :, None] * widened[..., None, :]
    products = products.reshape(widened.shape[:-1] + (FEAT * FEAT,))
    constant_term = jnp.ones(widened.shape[:-1] + (1,), jnp.float32)
    return jnp.concatenate(
        [constant_term, widened * FEAT ** (-0.25), products * (2.0 * FEAT) ** (-0.5)], -1
    ).astype(jnp.bfloat16)


def join_states(earlier, later):
    early_state, early_doc = earlier
    late_state, late_doc = later
    empty_late = late_doc[0] < 0.0
    matched = early_doc[0] == late_doc[0]
    joined = late_state + jnp.where(matched, early_state, jnp.zeros_like(early_state))
    return (jnp.where(empty_late, early_state, joined), jnp.where(empty_late, early_doc, late_doc))


def shards(tokens, doc_ids, w_feat, w_value, w_window, w_out):
    tok_rows = tokens.shape[0]
    head_count = w_value.shape[1] // HEAD_DIM
    highest = lax.Precision.HIGHEST
    zero_sums = (
        jnp.zeros((tok_rows, w_feat.shape[1]), jnp.float32),
        jnp.zeros((tok_rows, w_value.shape[1]), jnp.float32),
        jnp.zeros((tok_rows, w_window.shape[1]), jnp.float32),
    )
    column_piece = lax.all_gather(tokens, "head", axis=1, tiled=True)
    updated = []
    for running, weight in zip(zero_sums, (w_feat, w_value, w_window)):
        updated.append(jnp.dot(column_piece, weight, preferred_element_type=jnp.float32))
    feat_sum, value_sum, window_sum = tuple(updated)
    features = feat_sum.astype(jnp.bfloat16).reshape(tok_rows, head_count, 2 * FEAT)
    phi_query = feature_map(features[..., :FEAT])
    phi_key = feature_map(features[..., FEAT:])
    values_here = value_sum.astype(jnp.bfloat16).reshape(tok_rows, head_count, HEAD_DIM)
    window_proj = window_sum.astype(jnp.bfloat16).reshape(tok_rows, head_count, 2, HEAD_DIM)
    win_query = window_proj[:, :, 0]
    win_key = window_proj[:, :, 1]
    doc_float = doc_ids.astype(jnp.float32)
    positions = jnp.arange(tok_rows)
    allowed = (
        (doc_float[:, None] == doc_float[None, :]) & (positions[:, None] >= positions[None, :])
    ).astype(jnp.float32)
    scores = (
        jnp.einsum("thp,shp->hts", phi_query, phi_key, preferred_element_type=jnp.float32)
        * allowed[None]
    ).astype(jnp.bfloat16)
    inner = jnp.einsum("hts,shd->thd", scores, values_here, preferred_element_type=jnp.float32)
    keeps = doc_float == doc_float[-1]
    kept_keys = jnp.where(keeps[:, None, None], phi_key, jnp.zeros_like(phi_key))
    local_state = jnp.einsum(
        "shp,shd->hpd", kept_keys, values_here, preferred_element_type=jnp.float32
    )
    last_here = doc_float[tok_rows - 1 :]
    empty_state = jnp.zeros_like(local_state)
    incoming, in_doc = entering(
        (local_state, last_here),
        "ctx",
        join_states,
        (empty_state, jnp.full((1,), -1.0, jnp.float32)),
    )
    uses = doc_float == in_doc[0]
    carried = jnp.einsum("thp,hpd->thd", phi_query.astype(jnp.float32), incoming, precision=highest)
    linear_out = inner + jnp.where(uses[:, None, None], carried, jnp.zeros_like(carried))
    mean_square = jnp.mean(linear_out * linear_out, -1, keepdims=True)
    normed = linear_out * lax.rsqrt(mean_square + 1e-05)
    tail_key, tail_value, tail_doc = shifted(
        (
            win_key[tok_rows - WIN :],
            values_here[tok_rows - WIN :],
            (doc_float[tok_rows - WIN :] + 1.0).astype(jnp.bfloat16),
        ),
        "ctx",
        1,
    )
    keys_all = jnp.concatenate([tail_key, win_key], 0)
    values_cat = jnp.concatenate([tail_value, values_here], 0)
    docs_cat = jnp.concatenate([tail_doc.astype(jnp.float32) - 1.0, doc_float], 0)
    key_pos = jnp.arange(WIN + tok_rows)
    within = (
        (key_pos[None, :] > positions[:, None])
        & (key_pos[None, :] <= positions[:, None] + WIN)
        & (docs_cat[None, :] == doc_float[:, None])
    )
    logits = jnp.einsum(
        "thd,shd->hts", win_query, keys_all, preferred_element_type=jnp.float32
    ) * HEAD_DIM ** (-0.5)
    logits = jnp.where(within[None], logits, -1e30)
    top_logit = jnp.max(logits, -1, keepdims=True)
    weights = jnp.exp(logits - top_logit) * within[None].astype(jnp.float32)
    probs = (weights / jnp.sum(weights, -1, keepdims=True)).astype(jnp.bfloat16)
    window_out = jnp.einsum("hts,shd->thd", probs, values_cat, preferred_element_type=jnp.float32)
    mixed = (normed + window_out).astype(jnp.bfloat16).reshape(tok_rows, head_count * HEAD_DIM)
    summed = lax.psum_scatter(
        lax.dot_general(
            w_out, mixed, (((0,), (1,)), ((), ())), preferred_element_type=jnp.float32
        ).astype(jnp.bfloat16),
        "head",
        scatter_dimension=0,
        tiled=True,
    ).astype(jnp.float32)
    return summed.T.astype(jnp.bfloat16)


def solution(mesh):
    return jax.shard_map(
        shards,
        mesh=mesh,
        in_specs=(
            P("ctx", "head"),
            P("ctx"),
            P(None, "head"),
            P(None, "head"),
            P(None, "head"),
            P("head", None),
        ),
        out_specs=P("ctx", "head"),
        check_vma=False,
    )
```

profile of v0, /device:TPU:2, one launch (start us, length us, event | category | flops | bytes accessed | tf_op | source)
XLA Modules:
  0.0 281.5 jit_solution(10411707166912773014)
XLA Ops:
  8.6 1.2 dynamic-slice
  9.9 1.3 dynamic-update-slice
  11.2 3.5 %collective-permute-start.1 = (bf16[64]{0:T(256)(128)(2,1)S(1)}, bf16[64]{0:T(256)(128)(2,1)S(1)}, u32[]{:S(2)}, u32[]{:S(2)}) collective-permute-start(bf16[64]{0:T(256)(128)(2,1)S(1)} %add_convert_fusion), channel_id=1, source_target_pairs={{0,16},{16,32},{32,48},{48,64},{64,80},{80,96},{96,112},{112,128},... | collective-permute-start | bytes 392 | tf_op jit(solution)/shard_map/ppermute | solution.py:34
  14.7 33.2 %all-reduce = bf16[16]{0:T(256)(128)(2,1)S(1)} all-reduce(bf16[16]{0:T(256)(128)(2,1)S(1)} %dynamic-update-slice), channel_id=2, replica_groups=mesh['ctx'=16,'head'=16] {'ctx'}, use_global_device_ids=true, to_apply=%add | all-reduce | flops 16 | bytes 64
  48.6 1.3 broadcast_compare_fusion.1
  49.9 2.5 fusion.12
  52.4 23.7 %all-gather.5.cloned.1.call-done = bf16[1024,4096]{1,0:T(8,128)(2,1)} async-done(((bf16[1024,256]{1,0:T(8,128)(2,1)}), bf16[1024,4096]{1,0:T(8,128)(2,1)}) %all-gather.5.cloned.1.call-update) | async-done | bytes 8388624 | tf_op jit(solution)/shard_map/all_gather | solution.py:65
  76.1 6.2 %convolution_convert_fusion.3 = bf16[1024,64]{0,1:T(8,128)(2,1)S(1)} fusion(bf16[1024,4096]{1,0:T(8,128)(2,1)} %all-gather.5.cloned.1.call-done, bf16[4096,64]{0,1:T(8,128)(2,1)S(1)} %copy-done.6), kind=kOutput, calls=%fused_computation.36 | convolution fusion | flops 536936448 | bytes 9043968 | tf_op jit(solution)/shard_map/dot_general | solution.py:68
  82.9 1.0 copy-done.11
  83.9 2.3 convolution_convert_fusion.1
  86.3 0.8 copy-done.5
  87.0 1.2 convolution_convert_fusion.2
  88.4 3.5 %fusion.6 = (pred[1024,1088]{0,1:T(8,128)(4,1)}, f32[1024,1088]{0,1:T(8,128)}) fusion(f32[1024]{0:T(1024)S(1)} %convert_element_type.84, s32[1024]{0:T(1024)S(1)} %iota_add_fusion, f32[1088]{0:T(1024)S(1)} %pad_maximum_fusion.12), kind=kLoop, calls=%fused_computation.15 | loop fusion | flops 6684672 | bytes 5583104 | tf_op jit(solution)/shard_map/and | solution.py:119
  92.0 7.3 %convolution_convert_fusion = bf16[1024,512]{0,1:T(8,128)(2,1)S(1)} fusion(bf16[1024,4096]{1,0:T(8,128)(2,1)} %all-gather.5.cloned.1.call-done, bf16[4096,512]{1,0:T(8,128)(2,1)S(1)} %copy-done.10), kind=kOutput, calls=%fused_computation.26 | convolution fusion | flops 4295491584 | bytes 13631488 | tf_op jit(solution)/shard_map/dot_general | solution.py:68
  99.3 1.0 copy-done.8
  100.5 3.4 %collective-permute-start.2 = (bf16[64,2,128]{2,0,1:T(8,128)(2,1)S(1)}, bf16[64,2,128]{2,0,1:T(8,128)(2,1)S(1)}, u32[]{:S(2)}, u32[]{:S(2)}) collective-permute-start(bf16[64,2,128]{2,0,1:T(8,128)(2,1)S(1)} %bitcast.88), channel_id=1, source_target_pairs={{0,16},{16,32},{32,48},{48,64},{64,80},{80,96},{96,112},{112,128},... | collective-permute-start | bytes 98312 | tf_op jit(solution)/shard_map/ppermute | solution.py:34
  103.9 0.8 copy_bitcast_fusion.1
  104.7 3.6 %collective-permute-start = (bf16[64,2,128]{2,0,1:T(8,128)(2,1)S(1)}, bf16[64,2,128]{2,0,1:T(8,128)(2,1)}, u32[]{:S(2)}, u32[]{:S(2)}) collective-permute-start(bf16[64,2,128]{2,0,1:T(8,128)(2,1)S(1)} %copy_bitcast_fusion.1), channel_id=1, source_target_pairs={{0,16},{16,32},{32,48},{48,64},{64,80},{80,96},{96,112},{112,128},... | collective-permute-start | bytes 98312 | tf_op jit(solution)/shard_map/ppermute | solution.py:34
  108.2 2.0 copy_bitcast_fusion
  110.2 7.8 %fusion.9 = f32[2,128,1024]{2,1,0:T(8,128)} fusion(f32[1024,1024]{1,0:T(8,128)} %fusion.12, bf16[1024,2,256]{0,2,1:T(8,128)(2,1)} %bitcast.81, bf16[1024,2,16]{0,2,1:T(8,128)(2,1)S(1)} %get-tuple-element.54, bf16[1024,2,256]{0,2,1:T(8,128)(2,1)S(1)} %bitcast.78, bf16[1024,2,16]{0,2,1:T(8,128)(2,1)S(1)} %get-tuple-element.53, ...), kind=kOutput, calls=%fused_computation.18 | convolution fusion | flops 1692819456 | bytes 7995938 | tf_op jit(solution)/shard_map/hts,shd->thd/dot_general | solution.py:86
  118.0 1.1 slice.46
  119.4 10.6 %fusion.45 = (f32[2,1024]{1,0:T(2,128)S(1)}, f32[2,1024,1088]{1,2,0:T(8,128)}) fusion(f32[1024,1088]{0,1:T(8,128)} %get-tuple-element.58, pred[1024,1088]{0,1:T(8,128)(4,1)} %get-tuple-element.57, bf16[1024,2,2,128]{0,3,2,1:T(8,128)(2,1)} %bitcast.86, bf16[1024,2,128]{2,0,1:T(8,128)(2,1)S(1)} %bitcast.82, bf16[64,2,128]{2,0,1:T(8,128)(2,1)S(1)} %collective-permute-done.2), kind=kOutput, calls=%fused_computation.77 | convolution fusion | flops 582681664 | bytes 15572992 | tf_op jit(solution)/shard_map/sub | solution.py:128
  130.0 7.5 %all-gather.7.cloned.1.call-done = bf16[32,273,128]{2,1,0:T(8,128)(2,1)} async-done(((bf16[2,273,128]{2,1,0:T(8,128)(2,1)}), bf16[32,273,128]{2,1,0:T(8,128)(2,1)}) %all-gather.7.cloned.1.call-update) | async-done | bytes 2236432 | tf_op jit(solution)/shard_map/all_gather | solution.py:14
  137.5 14.7 %while.12 = (s32[]{:T(128)}, f32[2,273,128]{2,1,0:T(8,128)S(1)}, f32[1]{0:T(128)}, s32[]{:T(128)}, bf16[16,1]{0,1:T(2,128)(2,1)S(1)}, /*index=5*/bf16[16,2,273,1...) while((s32[]{:T(128)}, f32[2,273,128]{2,1,0:T(8,128)S(1)}, f32[1]{0:T(128)}, s32[]{:T(128)}, ...), condition=%wide.region_1.2_spmd, body=%wide.region_0.1_spmd.sunk | while | flops 279560 | bytes 699054 | solution.py:28
  139.4 1.1 fusion.59
  143.1 1.1 fusion.59
  146.7 1.1 fusion.59
  150.3 1.1 fusion.59
  152.3 2.6 multiply_reduce_fusion
  154.9 4.6 %fusion.19 = bf16[1024,2,128]{0,2,1:T(8,128)(2,1)S(1)} fusion(f32[2,1024,1088]{1,2,0:T(8,128)} %get-tuple-element.60, f32[2,1024]{1,0:T(2,128)S(1)} %get-tuple-element.59, f32[1024,2,128]{0,2,1:T(8,128)S(1)} %get-tuple-element.62, bf16[1024,2,128]{2,0,1:T(8,128)(2,1)S(1)} %copy-done.7, bf16[64,2,128]{2,0,1:T(8,128)(2,1)} %collective-permute-done, ...), kind=kOutput, calls=%fused_computation.32 | convolution fusion | flops 576782336 | bytes 11059200 | tf_op jit(solution)/shard_map/hts,shd->thd/dot_general | solution.py:130
  159.5 5.6 %convert_bitcast_fusion = bf16[4096,1024]{0,1:T(8,128)(2,1)} fusion(bf16[1024,256]{0,1:T(8,128)(2,1)S(1)} %bitcast.83, bf16[256,4096]{1,0:T(8,128)(2,1)S(1)} %copy-done), kind=kOutput, calls=%fused_computation.7 | convolution fusion | flops 2151677952 | bytes 11010048 | tf_op jit(solution)/shard_map/dot_general | solution.py:133
  165.2 109.8 %reduce-scatter.2.cloned.1.call-done = bf16[256,1024]{0,1:T(8,128)(2,1)} async-done(((bf16[4096,1024]{0,1:T(8,128)(2,1)}), bf16[256,1024]{0,1:T(8,128)(2,1)}) %reduce-scatter.2.cloned.1.call-update) | async-done | bytes 524304 | tf_op jit(solution)/shard_map/reduce_scatter | solution.py:132
  (52 shorter events, 6.3 us)
Async XLA Ops:
  6.5 153.0 %copy-start = (bf16[256,4096]{1,0:T(8,128)(2,1)S(1)}, bf16[256,4096]{1,0:T(8,128)(2,1)}, u32[]{:S(2)}) copy-start(bf16[256,4096]{1,0:T(8,128)(2,1)} %param.13) | copy-start | bytes 6291460
  6.5 69.6 %copy-start.6 = (bf16[4096,64]{0,1:T(8,128)(2,1)S(1)}, bf16[4096,64]{0,1:T(8,128)(2,1)}, u32[]{:S(2)}) copy-start(bf16[4096,64]{0,1:T(8,128)(2,1)} %param.10) | copy-start | bytes 1572868
  6.5 69.6 %all-gather.5.cloned.1.call-start = ((), (), s32[]{:S(2)}) async-start(), calls=%async_computation.1 | async-start | bytes 8912896 | tf_op jit(solution)/shard_map/all_gather | solution.py:65
  7.3 130.2 %all-gather.7.cloned.1.call-start = ((), (), s32[]{:S(2)}) async-start(), calls=%async_computation.3 | async-start | bytes 2437120 | tf_op jit(solution)/shard_map/all_gather | solution.py:14
  11.2 77.1 %collective-permute-start.1 = (bf16[64]{0:T(256)(128)(2,1)S(1)}, bf16[64]{0:T(256)(128)(2,1)S(1)}, u32[]{:S(2)}, u32[]{:S(2)}) collective-permute-start(bf16[64]{0:T(256)(128)(2,1)S(1)} %add_convert_fusion), channel_id=1, source_target_pairs={{0,16},{16,32},{32,48},{48,64},{64,80},{80,96},{96,112},{112,128},... | collective-permute-start | bytes 392 | tf_op jit(solution)/shard_map/ppermute | solution.py:34
  76.1 6.8 %copy-start.1 = (bf16[1024,4096]{1,0:T(8,128)(2,1)S(1)}, bf16[1024,4096]{1,0:T(8,128)(2,1)}, u32[]{:S(2)}) copy-start(bf16[1024,4096]{1,0:T(8,128)(2,1)} %all-gather.5.cloned.1.call-done) | copy-start | bytes 25165828
  82.3 1.6 copy-start.11
  83.9 2.4 copy-start.4
  83.9 26.3 %copy-start.2 = (bf16[1024,2,16,16]{0,3,2,1:T(8,128)(2,1)}, bf16[1024,2,16,16]{0,3,2,1:T(8,128)(2,1)S(1)}, u32[]{:S(2)}) copy-start(bf16[1024,2,16,16]{0,3,2,1:T(8,128)(2,1)S(1)} %get-tuple-element.64) | copy-start | bytes 3145732
  86.2 0.8 copy-start.5
  88.3 186.7 %reduce-scatter.2.cloned.1.call-start = ((), (), s32[]{:S(2)}) async-start(), calls=%async_computation.2 | async-start | bytes 8912896 | tf_op jit(solution)/shard_map/reduce_scatter | solution.py:132
  88.4 3.5 %copy-start.10 = (bf16[4096,512]{1,0:T(8,128)(2,1)S(1)}, bf16[4096,512]{1,0:T(8,128)(2,1)}, u32[]{:S(2)}) copy-start(bf16[4096,512]{1,0:T(8,128)(2,1)} %param.12) | copy-start | bytes 12582916
  99.3 1.0 copy-start.8
  100.5 18.9 %collective-permute-start.2 = (bf16[64,2,128]{2,0,1:T(8,128)(2,1)S(1)}, bf16[64,2,128]{2,0,1:T(8,128)(2,1)S(1)}, u32[]{:S(2)}, u32[]{:S(2)}) collective-permute-start(bf16[64,2,128]{2,0,1:T(8,128)(2,1)S(1)} %bitcast.88), channel_id=1, source_target_pairs={{0,16},{16,32},{32,48},{48,64},{64,80},{80,96},{96,112},{112,128},... | collective-permute-start | bytes 98312 | tf_op jit(solution)/shard_map/ppermute | solution.py:34
  104.7 50.3 %collective-permute-start = (bf16[64,2,128]{2,0,1:T(8,128)(2,1)S(1)}, bf16[64,2,128]{2,0,1:T(8,128)(2,1)}, u32[]{:S(2)}, u32[]{:S(2)}) collective-permute-start(bf16[64,2,128]{2,0,1:T(8,128)(2,1)S(1)} %copy_bitcast_fusion.1), channel_id=1, source_target_pairs={{0,16},{16,32},{32,48},{48,64},{64,80},{80,96},{96,112},{112,128},... | collective-permute-start | bytes 98312 | tf_op jit(solution)/shard_map/ppermute | solution.py:34
  129.9 22.3 %copy-start.9 = (s32[1024]{0:T(1024)S(1)}, s32[1024]{0:T(1024)}, u32[]{:S(2)}) copy-start(s32[1024]{0:T(1024)} %param.9) | copy-start | bytes 12292
  130.0 22.3 %copy-start.3 = (bf16[1024,2,16,16]{0,3,2,1:T(8,128)(2,1)S(1)}, bf16[1024,2,16,16]{0,3,2,1:T(8,128)(2,1)}, u32[]{:S(2)}) copy-start(bf16[1024,2,16,16]{0,3,2,1:T(8,128)(2,1)} %copy-done.2) | copy-start | bytes 3145732
  152.3 2.7 copy-start.7
Sparse Core Ops, SparseCore 0:
  9.1 66.9 all-gather.4
  88.4 49.0 all-gather.6
  165.3 109.6 reduce-scatter.1
where the time goes:
time: 283 us; the launch traced here: 282 us
  waiting for transfers between devices  142 us (50%)
  matrix products  48.2 us (17%)
  blocking collectives  33.2 us (12%)
  between operations  13.4 us (5%)
  local copies, waits for them, and re-layouts  13.2 us (5%)
  other arithmetic  13.1 us (5%)
  starting transfers between devices  10.5 us (4%)
  loops' own time  8.18 us (3%)
    reduce_scatter x1, waiting for transfers between devices, shards(): lax.psum_scatter(lax.dot_general(w_out, mixed, (((0,), (1,)), ((), ())),...  110 us
    unnamed x1, blocking collectives  33.2 us
    all_gather x1, waiting for transfers between devices, shards(): column_piece = lax.all_gather(tokens, 'head', axis=1, tiled=True)  23.7 us
    dot_general x3, matrix products, shards(): jnp.dot(column_piece, weight, preferred_element_type=jnp.float32)  15.8 us
    sub x1, matrix products, shards(): weights = jnp.exp(logits - top_logit) * within[None].astype(jnp.float32)  10.6 us
    ppermute x3, starting transfers between devices, shifted(): return lax.ppermute(x, axis, pairs)  10.4 us
    another operation x1, loops' own time, entering(): return lax.fori_loop(0, place, one, state)  8.18 us
    dot_general x1, matrix products, shards(): jnp.einsum('hts,shd->thd', scores, values_here, preferred_element_type=jn...  7.79 us
  transfers between devices with their start and end apart: 6, of which 3 were waited for; matrix products, arithmetic and copies ran while one was open for 22% of the time, Pallas kernels for 0%

commit v1 on v0

--- a/solution.py
+++ b/solution.py
@@ -62,7 +62,12 @@
         jnp.zeros((tok_rows, w_value.shape[1]), jnp.float32),
         jnp.zeros((tok_rows, w_window.shape[1]), jnp.float32),
     )
-    column_piece = lax.all_gather(tokens, "head", axis=1, tiled=True)
+    column_piece = jnp.concatenate(
+        jax.lax.all_to_all(
+            jnp.stack([tokens for _ in range(jax.lax.psum(1, "head"))], axis=0), "head", 0, 0
+        ),
+        axis=1,
+    )
     updated = []
     for running, weight in zip(zero_sums, (w_feat, w_value, w_window)):
         updated.append(jnp.dot(column_piece, weight, preferred_element_type=jnp.float32))

time: 283 us -> 432 us (1.53)
  waiting for transfers between devices: 142 us -> 280 us
  starting transfers between devices: 10.5 us -> 16.5 us
    all_to_all x0 -> x1, waiting for transfers between devices: none -> 174 us  [shards(): jax.lax.all_to_all(jnp.stack([tokens for _ in range(jax.lax.psum(1, 'head...]
    all_gather x1 -> x0, waiting for transfers between devices: 23.7 us -> none  [shards(): column_piece = lax.all_gather(tokens, 'head', axis=1, tiled=True)]
    all_to_all x0 -> x1, starting transfers between devices: none -> 8.75 us  [shards(): jax.lax.all_to_all(jnp.stack([tokens for _ in range(jax.lax.psum(1, 'head...]
    all_gather x1, waiting for transfers between devices: 7.53 us -> 0.01 us  [entering(): lax.all_gather(a.astype(kind), axis)]
  transfers between devices with their start and end apart: 6 -> 6, of which waited for: 3 -> 2; matrix products, arithmetic and copies ran while one was open for 22% -> 14% of each run, Pallas kernels for 0% -> 0%
where the time goes in v1:
time: 432 us; the launch traced here: 431 us
  waiting for transfers between devices  280 us (65%)
  matrix products  50.7 us (12%)
  blocking collectives  34.8 us (8%)
  starting transfers between devices  16.5 us (4%)
  local copies, waits for them, and re-layouts  15.5 us (4%)
  between operations  13.7 us (3%)
  other arithmetic  12.7 us (3%)
  loops' own time  7.25 us (2%)
    all_to_all x1, waiting for transfers between devices, shards(): jax.lax.all_to_all(jnp.stack([tokens for _ in range(jax.lax.psum(1, 'head...  174 us
    reduce_scatter x1, waiting for transfers between devices, shards(): lax.psum_scatter(lax.dot_general(w_out, mixed, (((0,), (1,)), ((), ())),...  106 us
    unnamed x1, blocking collectives  34.8 us
    dot_general x3, matrix products, shards(): jnp.dot(column_piece, weight, preferred_element_type=jnp.float32)  18.2 us
    sub x1, matrix products, shards(): weights = jnp.exp(logits - top_logit) * within[None].astype(jnp.float32)  10.6 us
    all_to_all x1, starting transfers between devices, shards(): jax.lax.all_to_all(jnp.stack([tokens for _ in range(jax.lax.psum(1, 'head...  8.75 us
  transfers between devices with their start and end apart: 6, of which 2 were waited for; matrix products, arithmetic and copies ran while one was open for 14% of the time, Pallas kernels for 0%

profile of v1, /device:TPU:2, one launch (start us, length us, event | category | flops | bytes accessed | tf_op | source)
XLA Modules:
  0.0 431.2 jit_solution(17886107794129457957)
XLA Ops:
  6.5 1.4 copy.22
  7.9 4.3 stack.2
  12.2 8.8 %all-to-all-start = ((bf16[16,1024,256]{1,2,0:T(8,128)(2,1)}), bf16[16,1024,256]{1,2,0:T(8,128)(2,1)}, u32[]{:S(2)}, u32[]{:S(2)}) async-start(bf16[16,1024,256]{1,2,0:T(8,128)(2,1)} %stack.2), calls=%async_computation | async-start | bytes 16777216 | tf_op jit(solution)/shard_map/all_to_all | solution.py:66
  21.2 3.6 collective-permute-start.1
  24.8 0.6 slice.34
  26.6 1.3 dynamic-update-slice
  28.5 2.5 fusion.12
  31.1 174.1 %all-to-all-done = bf16[16,1024,256]{1,2,0:T(8,128)(2,1)} async-done(((bf16[16,1024,256]{1,2,0:T(8,128)(2,1)}), bf16[16,1024,256]{1,2,0:T(8,128)(2,1)}, u32[]{:S(2)}, u32[]{:S(2)}) %all-to-all-start) | async-done | bytes 8388640 | tf_op jit(solution)/shard_map/all_to_all | solution.py:66
  205.2 5.1 %convolution_convert_fusion.3 = bf16[1024,64]{0,1:T(8,128)(2,1)S(1)} fusion(bf16[4096,64]{0,1:T(8,128)(2,1)S(1)} %copy-done.2, bf16[1024,4096]{0,1:T(8,128)(2,1)} %bitcast.6), kind=kOutput, calls=%fused_computation.36 | convolution fusion | flops 536936448 | bytes 9043968 | tf_op jit(solution)/shard_map/dot_general | solution.py:73
  210.4 5.8 %convolution_convert_fusion.1 = bf16[1024,256]{1,0:T(8,128)(2,1)S(1)} fusion(bf16[1024,4096]{0,1:T(8,128)(2,1)} %bitcast.6, bf16[4096,256]{1,0:T(8,128)(2,1)S(1)} %copy-done.1), kind=kOutput, calls=%fused_computation.33 | convolution fusion | flops 2147745792 | bytes 11010048 | tf_op jit(solution)/shard_map/dot_general | solution.py:73
  216.2 1.5 multiply_convert_fusion.2
  217.7 1.0 copy-done.4
  218.7 1.2 convolution_convert_fusion.2
  220.0 34.8 %all-reduce = bf16[16]{0:T(256)(128)(2,1)S(1)} all-reduce(bf16[16]{0:T(256)(128)(2,1)S(1)} %dynamic-update-slice), channel_id=2, replica_groups=mesh['ctx'=16,'head'=16] {'ctx'}, use_global_device_ids=true, to_apply=%add | all-reduce | flops 16 | bytes 64
  254.8 3.6 fusion.6
  258.4 7.3 %convolution_convert_fusion = bf16[1024,512]{0,1:T(8,128)(2,1)S(1)} fusion(bf16[1024,4096]{0,1:T(8,128)(2,1)} %bitcast.6, bf16[4096,512]{1,0:T(8,128)(2,1)S(1)} %copy-done.8), kind=kOutput, calls=%fused_computation.26 | convolution fusion | flops 4295491584 | bytes 13631488 | tf_op jit(solution)/shard_map/dot_general | solution.py:73
  265.7 1.0 copy-done.6
  266.9 1.9 collective-permute-start.2
  268.9 2.1 collective-permute-start
  271.0 0.8 copy_bitcast_fusion
  271.8 7.9 %fusion.9 = f32[2,128,1024]{2,1,0:T(8,128)} fusion(f32[1024,1024]{1,0:T(8,128)} %fusion.12, bf16[1024,2,256]{0,2,1:T(8,128)(2,1)} %bitcast.84, bf16[1024,2,16]{0,2,1:T(8,128)(2,1)S(1)} %get-tuple-element.54, bf16[1024,2,256]{0,2,1:T(8,128)(2,1)} %bitcast.81, bf16[1024,2,16]{0,2,1:T(8,128)(2,1)S(1)} %get-tuple-element.53, bf16[273]{0:T(512)(128)(2,1)S(1)} %pad.9.clone, ...), kind=kOutput, calls=%fused_computation.18 | convolution fusion | flops 1692819456 | bytes 7995938 | tf_op jit(solution)/shard_map/hts,shd->thd/dot_general | solution.py:91
  279.8 1.1 slice.46
  281.1 10.6 %fusion.45 = (f32[2,1024]{1,0:T(2,128)S(1)}, f32[2,1024,1088]{1,2,0:T(8,128)}) fusion(f32[1024,1088]{0,1:T(8,128)} %get-tuple-element.58, pred[1024,1088]{0,1:T(8,128)(4,1)} %get-tuple-element.57, bf16[1024,2,2,128]{0,3,2,1:T(8,128)(2,1)} %bitcast.89, bf16[1024,2,128]{2,0,1:T(8,128)(2,1)S(1)} %bitcast.85, bf16[64,2,128]{2,0,1:T(8,128)(2,1)S(1)} %collective-permute-done.2), kind=kOutput, calls=%fused_computation.77 | convolution fusion | flops 582681664 | bytes 15572992 | tf_op jit(solution)/shard_map/sub | solution.py:133
  291.7 13.7 %while.12 = (s32[]{:T(128)}, f32[2,273,128]{2,1,0:T(8,128)S(1)}, f32[1]{0:T(128)}, s32[]{:T(128)}, bf16[16,1]{0,1:T(2,128)(2,1)S(1)}, /*index=5*/bf16[16,2,273,1...) while((s32[]{:T(128)}, f32[2,273,128]{2,1,0:T(8,128)S(1)}, f32[1]{0:T(128)}, s32[]{:T(128)}, ...), condition=%wide.region_1.2_spmd, body=%wide.region_0.1_spmd.sunk | while | flops 279560 | bytes 699054 | solution.py:28
  293.4 1.1 fusion.59
  296.8 1.1 fusion.59
  300.2 1.1 fusion.59
  303.6 1.1 fusion.59
  305.5 2.6 multiply_reduce_fusion
  308.1 4.6 %fusion.19 = bf16[1024,2,128]{0,2,1:T(8,128)(2,1)S(1)} fusion(f32[2,1024,1088]{1,2,0:T(8,128)} %get-tuple-element.60, f32[2,1024]{1,0:T(2,128)S(1)} %get-tuple-element.59, f32[1024,2,128]{0,2,1:T(8,128)S(1)} %get-tuple-element.62, bf16[1024,2,128]{2,0,1:T(8,128)(2,1)S(1)} %copy-done.5, bf16[64,2,128]{2,0,1:T(8,128)(2,1)} %collective-permute-done, ...), kind=kOutput, calls=%fused_computation.32 | convolution fusion | flops 576782336 | bytes 11059200 | tf_op jit(solution)/shard_map/hts,shd->thd/dot_general | solution.py:135
  312.7 5.6 %convert_bitcast_fusion = bf16[4096,1024]{0,1:T(8,128)(2,1)} fusion(bf16[1024,256]{0,1:T(8,128)(2,1)S(1)} %bitcast.86, bf16[256,4096]{1,0:T(8,128)(2,1)S(1)} %copy-done), kind=kOutput, calls=%fused_computation.7 | convolution fusion | flops 2151677952 | bytes 11010048 | tf_op jit(solution)/shard_map/dot_general | solution.py:138
  318.4 106.0 %reduce-scatter.2.cloned.1.call-done = bf16[256,1024]{0,1:T(8,128)(2,1)} async-done(((bf16[4096,1024]{0,1:T(8,128)(2,1)}), bf16[256,1024]{0,1:T(8,128)(2,1)}) %reduce-scatter.2.cloned.1.call-update) | async-done | bytes 524304 | tf_op jit(solution)/shard_map/reduce_scatter | solution.py:137
  (49 shorter events, 4.9 us)
Async XLA Ops:
  6.5 306.2 %copy-start = (bf16[256,4096]{1,0:T(8,128)(2,1)S(1)}, bf16[256,4096]{1,0:T(8,128)(2,1)}, u32[]{:S(2)}) copy-start(bf16[256,4096]{1,0:T(8,128)(2,1)} %param.13) | copy-start | bytes 6291460
  12.2 8.8 %copy-start.7 = (s32[1024]{0:T(1024)S(1)}, s32[1024]{0:T(1024)}, u32[]{:S(2)}) copy-start(s32[1024]{0:T(1024)} %param.9) | copy-start | bytes 12292
  12.2 13.8 %copy-start.9 = (u32[256]{0:T(256)S(1)}, u32[256]{0:T(256)}, u32[]{:S(2)}) copy-start(u32[256]{0:T(256)} %constant.58) | copy-start | bytes 3076
  12.2 193.0 %all-to-all-start = ((bf16[16,1024,256]{1,2,0:T(8,128)(2,1)}), bf16[16,1024,256]{1,2,0:T(8,128)(2,1)}, u32[]{:S(2)}, u32[]{:S(2)}) async-start(bf16[16,1024,256]{1,2,0:T(8,128)(2,1)} %stack.2), calls=%async_computation | async-start | bytes 16777216 | tf_op jit(solution)/shard_map/all_to_all | solution.py:66
  21.0 184.2 %copy-start.2 = (bf16[4096,64]{0,1:T(8,128)(2,1)S(1)}, bf16[4096,64]{0,1:T(8,128)(2,1)}, u32[]{:S(2)}) copy-start(bf16[4096,64]{0,1:T(8,128)(2,1)} %param.10) | copy-start | bytes 1572868
  21.0 270.7 %all-gather.4.cloned.1.call-start = ((), (), s32[]{:S(2)}) async-start(), calls=%async_computation.3 | async-start | bytes 2437120 | tf_op jit(solution)/shard_map/all_gather | solution.py:14
  21.2 233.6 %collective-permute-start.1 = (bf16[64]{0:T(256)(128)(2,1)S(1)}, bf16[64]{0:T(256)(128)(2,1)S(1)}, u32[]{:S(2)}, u32[]{:S(2)}) collective-permute-start(bf16[64]{0:T(256)(128)(2,1)S(1)} %add_convert_fusion), channel_id=1, source_target_pairs={{0,16},{16,32},{32,48},{48,64},{64,80},{80,96},{96,112},{112,128},... | collective-permute-start | bytes 392 | tf_op jit(solution)/shard_map/ppermute | solution.py:34
  205.2 5.2 %copy-start.1 = (bf16[4096,256]{1,0:T(8,128)(2,1)S(1)}, bf16[4096,256]{1,0:T(8,128)(2,1)}, u32[]{:S(2)}) copy-start(bf16[4096,256]{1,0:T(8,128)(2,1)} %param.11) | copy-start | bytes 6291460
  217.7 1.0 copy-start.4
  219.9 204.5 %reduce-scatter.2.cloned.1.call-start = ((), (), s32[]{:S(2)}) async-start(), calls=%async_computation.2 | async-start | bytes 8912896 | tf_op jit(solution)/shard_map/reduce_scatter | solution.py:137
  254.8 3.6 copy-start.8
  265.7 1.0 copy-start.6
  266.9 14.2 %collective-permute-start.2 = (bf16[64,2,128]{2,0,1:T(8,128)(2,1)S(1)}, bf16[64,2,128]{2,0,1:T(8,128)(2,1)S(1)}, u32[]{:S(2)}, u32[]{:S(2)}) collective-permute-start(bf16[64,2,128]{2,0,1:T(8,128)(2,1)S(1)} %bitcast.91), channel_id=1, source_target_pairs={{0,16},{16,32},{32,48},{48,64},{64,80},{80,96},{96,112},{112,128},... | collective-permute-start | bytes 98312 | tf_op jit(solution)/shard_map/ppermute | solution.py:34
  268.9 39.2 %collective-permute-start = (bf16[64,2,128]{2,0,1:T(8,128)(2,1)S(1)}, bf16[64,2,128]{2,0,1:T(8,128)(2,1)}, u32[]{:S(2)}, u32[]{:S(2)}) collective-permute-start(bf16[64,2,128]{2,0,1:T(8,128)(2,1)S(1)} %copy_bitcast_fusion.1), channel_id=1, source_target_pairs={{0,16},{16,32},{32,48},{48,64},{64,80},{80,96},{96,112},{112,128},... | collective-permute-start | bytes 98312 | tf_op jit(solution)/shard_map/ppermute | solution.py:34
  291.7 13.8 %copy-start.3 = (bf16[1024,2,16,16]{0,3,2,1:T(8,128)(2,1)S(1)}, bf16[1024,2,16,16]{0,3,2,1:T(8,128)(2,1)}, u32[]{:S(2)}) copy-start(bf16[1024,2,16,16]{0,3,2,1:T(8,128)(2,1)} %get-tuple-element.64) | copy-start | bytes 3145732
  305.4 2.7 copy-start.5
Sparse Core Ops, SparseCore 0:
  220.0 49.1 all-gather.3
  318.5 105.8 reduce-scatter.1
